TPU v7x, 32 devices: a whole 2x2x4 slice. The times are simulated.
32 devices in a mesh: dp: 16 (over z, y, core), seq: 2 (over x).
Axes of the slice: x: 2, y: 2, z: 4, core: 2. Of those that a mesh axis runs over, the one named last changes fastest.
Arguments:
- pre_act: bfloat16 [16, 512, 768], P('dp', 'seq'), may hold values from -6 to 6
- trunk_grad: bfloat16 [16, 256, 768], P('dp', None, 'seq'), may hold values from -6 to 6
- conv_weight: bfloat16 [5, 768, 768], P(None, 'dp'), may hold values from -0.09375 to 0.09375
- pair_weight: bfloat16 [768, 768], replicated, may hold values from -0.21875 to 0.21875
- donor_slots: int32 [16, 2, 2, 128], P('dp', 'seq'), may hold values from 0 to 255
- accept_slots: int32 [16, 2, 2, 128], P('dp', 'seq'), may hold values from 0 to 255
- junction_grad: float32 [16, 2, 2, 128], P('dp', 'seq'), may hold values from -6 to 6
- pair_counts: int32 [16, 2, 2], P('dp'), may hold values from 0 to 128, as said below
Outputs:
- input_grad: bfloat16 [16, 512, 768], P('dp', 'seq')
- pair_grad: float32 [768, 768], replicated
Inputs may be any that keep to these rules, and one draw needn't show every extreme that they name: pair_counts is at most 128; in every sample some acceptor slab has 128 live slots from every donor slab.
All inputs are finite; a program needn't handle non-finite values.
Results may differ from a plain program's by a relative error of at most 0.0061.
Values may be sent and summed in bfloat16 or wider, within the bound.
A program may use at most 64 MiB of HBM per device.

v0:
```python
import math
import jax
import jax.numpy as jnp
from jax import lax
from jax.sharding import PartitionSpec as P


def with_halo(x, sides, width):
    for axis, dim in sides:
        size, length = (lax.axis_size(axis), x.shape[dim])
        up = [(i, (i + 1) % size) for i in range(size - 1)]
        down = [(j, i) for i, j in up]
        last = lax.slice_in_dim(x, length - width, length, axis=dim)
        first = lax.slice_in_dim(x, 0, width, axis=dim)
        before = lax.ppermute(last, axis, up)
        after = lax.ppermute(first, axis, down)
        x = jnp.concatenate([before, x, after], axis=dim)
    return x


def gelu_parts(values):
    normal_cdf = 0.5 * (1.0 + jax.scipy.special.erf(values / math.sqrt(2.0)))
    density = jnp.exp(-0.5 * values * values) / math.sqrt(2.0 * math.pi)
    return (values * normal_cdf, normal_cdf + values * density)


def per_device(
    pre_act,
    trunk_grad,
    conv_weight,
    pair_weight,
    donor_slots,
    accept_slots,
    junction_grad,
    pair_counts,
):
    seq_count = lax.axis_size("seq")
    my_slab = lax.axis_index("seq")
    slab_len = pre_act.shape[1]
    channels = pre_act.shape[2]
    slot_count = donor_slots.shape[3]
    kernel = conv_weight.shape[0]
    half = kernel // 2
    act_f, slope = gelu_parts(pre_act[0].astype(jnp.float32))
    act = act_f.astype(jnp.bfloat16)
    arrived = lax.all_to_all(trunk_grad, "seq", split_axis=1, concat_axis=2, tiled=True)
    pooled = jnp.repeat(arrived[0].astype(jnp.float32) * 0.5, 2, axis=0)
    send_index = donor_slots[0, 0].reshape(-1)
    outgoing = act[send_index].reshape(seq_count, slot_count, channels)
    incoming = lax.all_to_all(outgoing, "seq", split_axis=0, concat_axis=0, tiled=True)
    donor_rows = incoming.reshape(-1, channels)
    accept_index = accept_slots[0, 0].reshape(-1)
    counts_in = lax.dynamic_index_in_dim(pair_counts[0], my_slab, axis=1, keepdims=False)
    live = jnp.arange(slot_count, dtype=jnp.int32)[None, :] < counts_in[:, None]
    slot_w = jnp.where(live, junction_grad[0, 0], 0.0).reshape(-1)
    accept_rows = act[accept_index]
    weighted = (slot_w[:, None] * accept_rows.astype(jnp.float32)).astype(jnp.bfloat16)
    accept_term = (
        jnp.dot(donor_rows, pair_weight, preferred_element_type=jnp.float32) * slot_w[:, None]
    )
    donor_term = lax.dot_general(
        weighted, pair_weight, (((1,), (1,)), ((), ())), preferred_element_type=jnp.float32
    ).astype(jnp.bfloat16)
    pair_part = lax.dot_general(
        donor_rows, weighted, (((0,), (0,)), ((), ())), preferred_element_type=jnp.float32
    )
    returned = lax.all_to_all(
        donor_term.reshape(seq_count, slot_count, channels),
        "seq",
        split_axis=0,
        concat_axis=0,
        tiled=True,
    )
    act_grad = (
        pooled.at[accept_index]
        .add(accept_term)
        .at[send_index]
        .add(returned.reshape(-1, channels).astype(jnp.float32))
    )
    conv_grad = (act_grad * slope).astype(jnp.bfloat16)
    padded = with_halo(conv_grad[None], (("seq", 1),), half)[0]
    piece = lax.all_gather(conv_weight, "dp", axis=1, tiled=True)
    total = jnp.zeros((slab_len, piece.shape[1]), jnp.float32)
    for tap in range(kernel):
        window = padded[2 * half - tap : 2 * half - tap + slab_len]
        total = total + lax.dot_general(
            window, piece[tap], (((1,), (1,)), ((), ())), preferred_element_type=jnp.float32
        )
    input_grad = total.astype(jnp.bfloat16)
    pair_sum = lax.psum(pair_part, ("dp", "seq"))
    scale = 1.0 / math.sqrt(lax.axis_size("dp") * seq_count * seq_count * slot_count)
    return (input_grad[None], pair_sum * scale)


def solution(mesh):
    in_specs = (
        P("dp", "seq", None),
        P("dp", None, "seq"),
        P(None, "dp", None),
        P(),
        P("dp", "seq", None, None),
        P("dp", "seq", None, None),
        P("dp", "seq", None, None),
        P("dp", None, None),
    )
    out_specs = (P("dp", "seq", None), P())
    return jax.shard_map(
        per_device, mesh=mesh, in_specs=in_specs, out_specs=out_specs, check_vma=False
    )
```

profile of v0, /device:TPU:0, one launch (start us, length us, event | category | flops | bytes accessed | tf_op | source)
XLA Modules:
  0.0 200.0 jit_solution(1862598864620470224)
XLA Ops:
  8.0 0.0 copy-start
  8.0 1.3 fusion.6
  9.3 0.0 copy-start.4
  9.3 0.7 compare_select_fusion
  10.0 1.9 gather_fusion
  11.9 0.0 copy-start.5
  11.9 0.0 copy-start.6
  11.9 4.3 %all-to-all-start.1 = ((bf16[2,128,768]{2,1,0:T(8,128)(2,1)}), bf16[2,128,768]{2,1,0:T(8,128)(2,1)S(1)}, u32[]{:S(2)}, u32[]{:S(2)}) async-start(bf16[2,128,768]{2,1,0:T(8,128)(2,1)} %bitcast.9), calls=%async_computation.1 | async-start | bytes 786432 | tf_op jit(solution)/shard_map/all_to_all | solution.py:50
  16.3 0.0 all-reduce.2.cloned.1.call-start
  16.3 0.0 copy-done.4
  16.3 1.2 gather_fusion.1
  17.5 0.0 copy-done.5
  17.5 0.2 dynamic-slice_reduce_fusion
  17.7 0.0 copy-done.6
  17.7 0.1 bitcast_select_fusion
  17.8 5.8 %all-to-all-done.1 = bf16[2,128,768]{2,1,0:T(8,128)(2,1)S(1)} async-done(((bf16[2,128,768]{2,1,0:T(8,128)(2,1)}), bf16[2,128,768]{2,1,0:T(8,128)(2,1)S(1)}, u32[]{:S(2)}, u32[]{:S(2)}) %all-to-all-start.1) | async-done | bytes 393248 | tf_op jit(solution)/shard_map/all_to_all | solution.py:50
  23.6 0.0 copy-start.3
  23.6 2.0 fusion.26
  25.6 0.0 all-reduce.2.cloned.1.call-update
  25.6 0.0 all-gather.2.cloned.1.call-start
  25.6 0.5 all-gather.2.cloned.1.call-update
  26.2 0.0 copy-done.3
  26.2 0.3 copy.19
  26.5 0.5 broadcast.65
  27.0 1.8 reduce.2
  28.8 0.7 reshape.152
  29.5 3.4 %all-to-all-start = ((bf16[2,2,24576]{2,1,0:T(2,128)(2,1)}), bf16[2,2,24576]{2,1,0:T(2,128)(2,1)S(1)}, u32[]{:S(2)}, u32[]{:S(2)}) async-start(bf16[2,2,24576]{2,1,0:T(2,128)(2,1)} %reshape.152), calls=%async_computation | async-start | bytes 393216 | tf_op jit(solution)/shard_map/all_to_all | solution.py:46
  33.0 0.0 copy-done
  33.0 1.3 convolution_convert_fusion
  34.3 4.3 %all-to-all-done = bf16[2,2,24576]{2,1,0:T(2,128)(2,1)S(1)} async-done(((bf16[2,2,24576]{2,1,0:T(2,128)(2,1)}), bf16[2,2,24576]{2,1,0:T(2,128)(2,1)S(1)}, u32[]{:S(2)}, u32[]{:S(2)}) %all-to-all-start) | async-done | bytes 196640 | tf_op jit(solution)/shard_map/all_to_all | solution.py:46
  38.6 4.2 %all-to-all-start.2 = ((bf16[2,128,768]{2,1,0:T(8,128)(2,1)}), bf16[2,128,768]{2,1,0:T(8,128)(2,1)}, u32[]{:S(2)}, u32[]{:S(2)}) async-start(bf16[2,128,768]{2,1,0:T(8,128)(2,1)} %bitcast.13), calls=%async_computation.2 | async-start | bytes 786432 | tf_op jit(solution)/shard_map/all_to_all | solution.py:67
  42.8 0.2 reshape.153
  43.0 0.2 copy.15
  43.2 0.2 copy.16
  43.4 0.3 broadcast_in_dim.10
  43.7 0.5 reshape.111
  44.2 0.5 convolution_multiply_fusion
  44.7 0.0 copy-start.1
  44.7 2.5 %scatter_fusion = f32[256,768]{1,0:T(8,128)S(1)} fusion(f32[256,768]{1,0:T(8,128)S(1)} %reshape.111, s32[256]{0:T(256)S(1)} %bitcast.77, f32[256,768]{1,0:T(8,128)S(1)} %convolution_multiply_fusion), kind=kCustom, calls=%fused_computation.2 | custom fusion | flops 196608 | bytes 2360320 | tf_op jit(solution)/shard_map/scatter-add | solution.py:76
  47.3 2.6 %all-to-all-done.2 = bf16[2,128,768]{2,1,0:T(8,128)(2,1)} async-done(((bf16[2,128,768]{2,1,0:T(8,128)(2,1)}), bf16[2,128,768]{2,1,0:T(8,128)(2,1)}, u32[]{:S(2)}, u32[]{:S(2)}) %all-to-all-start.2) | async-done | bytes 393248 | tf_op jit(solution)/shard_map/all_to_all | solution.py:67
  49.9 3.0 %scatter_custom_fusion.1 = f32[256,768]{1,0:T(8,128)S(1)} fusion(f32[256,768]{1,0:T(8,128)S(1)} %scatter_fusion, s32[256]{0:T(256)S(1)} %bitcast.79, bf16[256,768]{1,0:T(8,128)(2,1)} %bitcast.27), kind=kCustom, calls=%fused_computation.33 | custom fusion | flops 393216 | bytes 1179648 | tf_op jit(solution)/shard_map/scatter-add | solution.py:78
  52.9 0.0 copy-done.1
  52.9 0.4 fusion.11
  53.3 1.3 collective-permute-start
  54.6 4.7 %collective-permute-start.1 = (bf16[1,2,768]{2,1,0:T(2,128)(2,1)S(1)}, bf16[1,2,768]{2,1,0:T(2,128)(2,1)S(1)}, u32[]{:S(2)}, u32[]{:S(2)}) collective-permute-start(bf16[1,2,768]{2,1,0:T(2,128)(2,1)S(1)} %get-tuple-element.2), channel_id=1, source_target_pairs={{0,1},{2,3},{4,5},{6,7},{8,9},{10,11},{12,13},{14,15},{16,17},{18,... | collective-permute-start | bytes 9224 | tf_op jit(solution)/shard_map/ppermute | solution.py:15
  59.3 123.8 %all-reduce.2.cloned.1.call-done = f32[768,768]{1,0:T(8,128)} async-done(((f32[768,768]{1,0:T(8,128)}), f32[768,768]{1,0:T(8,128)}) %all-reduce.2.cloned.1.call-update) | async-done | bytes 2359312 | tf_op jit(solution)/shard_map/psum | solution.py:90
  183.1 3.3 %broadcast_multiply_fusion = f32[768,768]{1,0:T(8,128)} fusion(f32[768,768]{1,0:T(8,128)} %all-reduce.2.cloned.1.call-done), kind=kLoop, calls=%fused_computation.23 | loop fusion | flops 589824 | bytes 4718592 | tf_op jit(solution)/shard_map/mul | solution.py:92
  186.4 0.0 collective-permute-done
  186.4 0.0 all-gather.2.cloned.1.call-done
  186.4 0.0 copy-start.2
  186.4 1.9 fusion.2
  188.3 1.9 convolution_add_fusion.3
  190.2 0.0 copy-done.2
  190.3 0.5 convolution_add_fusion.2
  190.8 0.0 collective-permute-done.1
  190.8 0.5 convolution_add_fusion.1
  191.3 1.3 fusion.1
  (5 shorter events, 0.1 us)
Async XLA Ops:
  8.0 25.0 %copy-start = (bf16[768,768]{1,0:T(8,128)(2,1)S(1)}, bf16[768,768]{1,0:T(8,128)(2,1)}, u32[]{:S(2)}) copy-start(bf16[768,768]{1,0:T(8,128)(2,1)} %param.11) | copy-start | bytes 3538948
  9.3 7.0 %copy-start.4 = (s32[1,1,2,128]{3,2,1,0:T(2,128)S(1)}, s32[1,1,2,128]{3,2,1,0:T(2,128)}, u32[]{:S(2)}) copy-start(s32[1,1,2,128]{3,2,1,0:T(2,128)} %param.13) | copy-start | bytes 3076
  11.9 5.6 %copy-start.5 = (s32[1,2,2]{2,1,0:T(2,128)S(1)}, s32[1,2,2]{2,1,0:T(2,128)}, u32[]{:S(2)}) copy-start(s32[1,2,2]{2,1,0:T(2,128)} %param.15) | copy-start | bytes 52
  11.9 5.8 %copy-start.6 = (f32[1,1,2,128]{3,2,1,0:T(2,128)S(1)}, f32[1,1,2,128]{3,2,1,0:T(2,128)}, u32[]{:S(2)}) copy-start(f32[1,1,2,128]{3,2,1,0:T(2,128)} %param.14) | copy-start | bytes 3076
  11.9 11.6 %all-to-all-start.1 = ((bf16[2,128,768]{2,1,0:T(8,128)(2,1)}), bf16[2,128,768]{2,1,0:T(8,128)(2,1)S(1)}, u32[]{:S(2)}, u32[]{:S(2)}) async-start(bf16[2,128,768]{2,1,0:T(8,128)(2,1)} %bitcast.9), calls=%async_computation.1 | async-start | bytes 786432 | tf_op jit(solution)/shard_map/all_to_all | solution.py:50
  16.3 166.8 %all-reduce.2.cloned.1.call-start = ((), (), s32[]{:S(2)}) async-start(), calls=%async_computation.4 | async-start | bytes 4718592 | tf_op jit(solution)/shard_map/psum | solution.py:90
  23.6 2.6 %copy-start.3 = (bf16[1,256,384]{2,1,0:T(8,128)(2,1)S(1)}, bf16[1,256,384]{2,1,0:T(8,128)(2,1)}, u32[]{:S(2)}) copy-start(bf16[1,256,384]{2,1,0:T(8,128)(2,1)} %param.9) | copy-start | bytes 589828
  25.6 160.8 %all-gather.2.cloned.1.call-start = ((), (), s32[]{:S(2)}) async-start(), calls=%async_computation.3 | async-start | bytes 6266880 | tf_op jit(solution)/shard_map/all_gather | solution.py:82
  29.5 9.0 %all-to-all-start = ((bf16[2,2,24576]{2,1,0:T(2,128)(2,1)}), bf16[2,2,24576]{2,1,0:T(2,128)(2,1)S(1)}, u32[]{:S(2)}, u32[]{:S(2)}) async-start(bf16[2,2,24576]{2,1,0:T(2,128)(2,1)} %reshape.152), calls=%async_computation | async-start | bytes 393216 | tf_op jit(solution)/shard_map/all_to_all | solution.py:46
  38.6 11.3 %all-to-all-start.2 = ((bf16[2,128,768]{2,1,0:T(8,128)(2,1)}), bf16[2,128,768]{2,1,0:T(8,128)(2,1)}, u32[]{:S(2)}, u32[]{:S(2)}) async-start(bf16[2,128,768]{2,1,0:T(8,128)(2,1)} %bitcast.13), calls=%async_computation.2 | async-start | bytes 786432 | tf_op jit(solution)/shard_map/all_to_all | solution.py:67
  44.7 8.2 %copy-start.1 = (bf16[1,256,768]{2,1,0:T(8,128)(2,1)S(1)}, bf16[1,256,768]{2,1,0:T(8,128)(2,1)}, u32[]{:S(2)}) copy-start(bf16[1,256,768]{2,1,0:T(8,128)(2,1)} %param.8) | copy-start | bytes 1179652
  53.3 133.1 %collective-permute-start = (bf16[1,2,768]{2,1,0:T(2,128)(2,1)S(1)}, bf16[1,2,768]{2,1,0:T(2,128)(2,1)S(1)}, u32[]{:S(2)}, u32[]{:S(2)}) collective-permute-start(bf16[1,2,768]{2,1,0:T(2,128)(2,1)S(1)} %get-tuple-element.3), channel_id=1, source_target_pairs={{1,0},{3,2},{5,4},{7,6},{9,8},{11,10},{13,12},{15,14},{17,16},{19,... | collective-permute-start | bytes 9224 | tf_op jit(solution)/shard_map/ppermute | solution.py:16
  54.6 136.2 %collective-permute-start.1 = (bf16[1,2,768]{2,1,0:T(2,128)(2,1)S(1)}, bf16[1,2,768]{2,1,0:T(2,128)(2,1)S(1)}, u32[]{:S(2)}, u32[]{:S(2)}) collective-permute-start(bf16[1,2,768]{2,1,0:T(2,128)(2,1)S(1)} %get-tuple-element.2), channel_id=1, source_target_pairs={{0,1},{2,3},{4,5},{6,7},{8,9},{10,11},{12,13},{14,15},{16,17},{18,... | collective-permute-start | bytes 9224 | tf_op jit(solution)/shard_map/ppermute | solution.py:15
  186.4 3.9 %copy-start.2 = (bf16[5,768,768]{2,1,0:T(8,128)(2,1)S(1)}, bf16[5,768,768]{2,1,0:T(8,128)(2,1)}, u32[]{:S(2)}) copy-start(bf16[5,768,768]{2,1,0:T(8,128)(2,1)} %all-gather.2.cloned.1.call-done) | copy-start | bytes 17694724
Sparse Core Ops, SparseCore 0:
  25.7 157.3 all-reduce.1
Sparse Core Ops, SparseCore 1:
  28.3 64.0 all-gather.1
where the time goes:
time: 200 us
  waiting for transfers between devices  137 us (68%)
  starting transfers between devices  18 us (9%)
  between operations  15.7 us (8%)
  other arithmetic  13.1 us (7%)
  matrix products  9.85 us (5%)
  local copies, waits for them, and re-layouts  6.27 us (3%)
    psum x1, waiting for transfers between devices, per_device(): pair_sum = lax.psum(pair_part, ('dp', 'seq'))  124 us
    dot_general x5, matrix products, per_device(): lax.dot_general(window, piece[tap], (((1,), (1,)), ((), ())), preferred_e...  6.13 us
    all_to_all x1, waiting for transfers between devices, per_device(): lax.all_to_all(outgoing, 'seq', split_axis=0, concat_axis=0, tiled=True)  5.81 us
    scatter-add x2, other arithmetic, per_device(): act_grad = pooled.at[accept_index].add(accept_term).at[send_index].add(re...  5.57 us
    ppermute x1, starting transfers between devices, with_halo(): before = lax.ppermute(last, axis, up)  4.72 us
    all_to_all x1, starting transfers between devices, per_device(): lax.all_to_all(outgoing, 'seq', split_axis=0, concat_axis=0, tiled=True)  4.34 us
    all_to_all x1, waiting for transfers between devices, per_device(): lax.all_to_all(trunk_grad, 'seq', split_axis=1, concat_axis=2, tiled=True)  4.32 us
    all_to_all x1, starting transfers between devices, per_device(): lax.all_to_all(donor_term.reshape(seq_count, slot_count, channels), 'seq'...  4.17 us
  transfers between devices with their start and end apart: 7, of which 4 were waited for; matrix products, arithmetic and copies ran while one was open for 11% of the time, Pallas kernels for 0%

commit v1 on v0

--- a/solution.py
+++ b/solution.py
@@ -87,7 +87,7 @@
             window, piece[tap], (((1,), (1,)), ((), ())), preferred_element_type=jnp.float32
         )
     input_grad = total.astype(jnp.bfloat16)
-    pair_sum = lax.psum(pair_part, ("dp", "seq"))
+    pair_sum = lax.psum(lax.psum(pair_part, "seq"), "dp")
     scale = 1.0 / math.sqrt(lax.axis_size("dp") * seq_count * seq_count * slot_count)
     return (input_grad[None], pair_sum * scale)
 

time: 200 us -> 272 us (1.36)
  waiting for transfers between devices: 137 us -> 210 us
    all_gather x1, waiting for transfers between devices: 0.01 us -> 58.1 us  [per_device(): piece = lax.all_gather(conv_weight, 'dp', axis=1, tiled=True)]
    psum x1 -> x2, waiting for transfers between devices: 124 us -> 141 us  [per_device(): pair_sum = lax.psum(lax.psum(pair_part, 'seq'), 'dp')]
  transfers between devices with their start and end apart: 7 -> 8, of which waited for: 4 -> 6; matrix products, arithmetic and copies ran while one was open for 11% -> 8% of each run, Pallas kernels for 0% -> 0%
where the time goes in v1:
time: 272 us; the launch traced here: 271 us
  waiting for transfers between devices  210 us (77%)
  starting transfers between devices  17.9 us (7%)
  between operations  14 us (5%)
  other arithmetic  13.1 us (5%)
  matrix products  9.85 us (4%)
  local copies, waits for them, and re-layouts  6.26 us (2%)
    psum x2, waiting for transfers between devices, per_device(): pair_sum = lax.psum(lax.psum(pair_part, 'seq'), 'dp')  141 us
    all_gather x1, waiting for transfers between devices, per_device(): piece = lax.all_gather(conv_weight, 'dp', axis=1, tiled=True)  58.1 us
    dot_general x5, matrix products, per_device(): lax.dot_general(window, piece[tap], (((1,), (1,)), ((), ())), preferred_e...  6.12 us
    all_to_all x1, waiting for transfers between devices, per_device(): lax.all_to_all(outgoing, 'seq', split_axis=0, concat_axis=0, tiled=True)  5.81 us
    scatter-add x2, other arithmetic, per_device(): act_grad = pooled.at[accept_index].add(accept_term).at[send_index].add(re...  5.57 us
  transfers between devices with their start and end apart: 8, of which 6 were waited for; matrix products, arithmetic and copies ran while one was open for 8% of the time, Pallas kernels for 0%

profile of v1, /device:TPU:0, one launch (start us, length us, event | category | flops | bytes accessed | tf_op | source)
XLA Modules:
  0.0 271.5 jit_solution(3508258621242941812)
XLA Ops:
  7.2 0.0 copy-start
  7.2 1.3 fusion.6
  8.5 0.0 copy-start.4
  8.5 0.7 compare_select_fusion
  9.2 1.9 gather_fusion
  11.1 0.0 copy-start.5
  11.1 0.0 copy-start.6
  11.1 4.3 %all-to-all-start.1 = ((bf16[2,128,768]{2,1,0:T(8,128)(2,1)}), bf16[2,128,768]{2,1,0:T(8,128)(2,1)S(1)}, u32[]{:S(2)}, u32[]{:S(2)}) async-start(bf16[2,128,768]{2,1,0:T(8,128)(2,1)} %bitcast.9), calls=%async_computation.1 | async-start | bytes 786432 | tf_op jit(solution)/shard_map/all_to_all | solution.py:50
  15.4 0.0 all-reduce.3.cloned.1.call-start
  15.4 0.0 copy-done.4
  15.5 1.2 gather_fusion.1
  16.7 0.0 copy-done.5
  16.7 0.2 dynamic-slice_reduce_fusion
  16.8 0.0 copy-done.6
  16.9 0.1 bitcast_select_fusion
  16.9 5.8 %all-to-all-done.1 = bf16[2,128,768]{2,1,0:T(8,128)(2,1)S(1)} async-done(((bf16[2,128,768]{2,1,0:T(8,128)(2,1)}), bf16[2,128,768]{2,1,0:T(8,128)(2,1)S(1)}, u32[]{:S(2)}, u32[]{:S(2)}) %all-to-all-start.1) | async-done | bytes 393248 | tf_op jit(solution)/shard_map/all_to_all | solution.py:50
  22.7 2.0 fusion.26
  24.7 0.0 copy-start.3
  24.7 0.0 all-reduce.3.cloned.1.call-update
  24.7 0.0 all-reduce.5.cloned.1.call-start
  24.8 69.3 %all-reduce.3.cloned.1.call-done = f32[768,768]{1,0:T(8,128)} async-done(((f32[768,768]{1,0:T(8,128)}), f32[768,768]{1,0:T(8,128)}) %all-reduce.3.cloned.1.call-update) | async-done | bytes 2359312 | tf_op jit(solution)/shard_map/psum | solution.py:90
  94.1 0.0 all-reduce.5.cloned.1.call-update
  94.1 0.0 all-gather.2.cloned.1.call-start
  94.2 0.7 all-gather.2.cloned.1.call-update
  94.9 0.0 copy-done.3
  94.9 0.3 copy.19
  95.2 0.5 broadcast.65
  95.7 1.8 reduce.2
  97.5 0.7 reshape.152
  98.2 3.4 %all-to-all-start = ((bf16[2,2,24576]{2,1,0:T(2,128)(2,1)}), bf16[2,2,24576]{2,1,0:T(2,128)(2,1)S(1)}, u32[]{:S(2)}, u32[]{:S(2)}) async-start(bf16[2,2,24576]{2,1,0:T(2,128)(2,1)} %reshape.152), calls=%async_computation | async-start | bytes 393216 | tf_op jit(solution)/shard_map/all_to_all | solution.py:46
  101.7 0.0 copy-done
  101.7 1.3 convolution_convert_fusion
  103.0 3.5 %all-to-all-done = bf16[2,2,24576]{2,1,0:T(2,128)(2,1)S(1)} async-done(((bf16[2,2,24576]{2,1,0:T(2,128)(2,1)}), bf16[2,2,24576]{2,1,0:T(2,128)(2,1)S(1)}, u32[]{:S(2)}, u32[]{:S(2)}) %all-to-all-start) | async-done | bytes 196640 | tf_op jit(solution)/shard_map/all_to_all | solution.py:46
  106.5 4.2 %all-to-all-start.2 = ((bf16[2,128,768]{2,1,0:T(8,128)(2,1)}), bf16[2,128,768]{2,1,0:T(8,128)(2,1)}, u32[]{:S(2)}, u32[]{:S(2)}) async-start(bf16[2,128,768]{2,1,0:T(8,128)(2,1)} %bitcast.13), calls=%async_computation.2 | async-start | bytes 786432 | tf_op jit(solution)/shard_map/all_to_all | solution.py:67
  110.7 0.2 reshape.153
  111.0 0.2 copy.15
  111.1 0.2 copy.16
  111.3 0.3 broadcast_in_dim.10
  111.6 0.5 reshape.111
  112.1 0.5 convolution_multiply_fusion
  112.6 0.0 copy-start.1
  112.6 2.5 scatter_fusion
  115.2 1.5 all-to-all-done.2
  116.6 3.0 %scatter_custom_fusion.1 = f32[256,768]{1,0:T(8,128)S(1)} fusion(f32[256,768]{1,0:T(8,128)S(1)} %scatter_fusion, s32[256]{0:T(256)S(1)} %bitcast.79, bf16[256,768]{1,0:T(8,128)(2,1)} %bitcast.27), kind=kCustom, calls=%fused_computation.33 | custom fusion | flops 393216 | bytes 1179648 | tf_op jit(solution)/shard_map/scatter-add | solution.py:78
  119.7 0.0 copy-done.1
  119.7 0.4 fusion.11
  120.1 1.3 collective-permute-start
  121.4 4.5 %collective-permute-start.1 = (bf16[1,2,768]{2,1,0:T(2,128)(2,1)S(1)}, bf16[1,2,768]{2,1,0:T(2,128)(2,1)S(1)}, u32[]{:S(2)}, u32[]{:S(2)}) collective-permute-start(bf16[1,2,768]{2,1,0:T(2,128)(2,1)S(1)} %get-tuple-element.2), channel_id=1, source_target_pairs={{0,1},{2,3},{4,5},{6,7},{8,9},{10,11},{12,13},{14,15},{16,17},{18,... | collective-permute-start | bytes 9224 | tf_op jit(solution)/shard_map/ppermute | solution.py:15
  125.9 71.4 %all-reduce.5.cloned.1.call-done = f32[768,768]{1,0:T(8,128)} async-done(((f32[768,768]{1,0:T(8,128)}), f32[768,768]{1,0:T(8,128)}) %all-reduce.5.cloned.1.call-update) | async-done | bytes 2359312 | tf_op jit(solution)/shard_map/psum | solution.py:90
  197.4 3.3 %broadcast_multiply_fusion = f32[768,768]{1,0:T(8,128)} fusion(f32[768,768]{1,0:T(8,128)} %all-reduce.5.cloned.1.call-done), kind=kLoop, calls=%fused_computation.23 | loop fusion | flops 589824 | bytes 4718592 | tf_op jit(solution)/shard_map/mul | solution.py:92
  200.6 0.0 collective-permute-done
  200.6 58.1 %all-gather.2.cloned.1.call-done = bf16[5,768,768]{2,1,0:T(8,128)(2,1)} async-done(((bf16[5,48,768]{2,1,0:T(8,128)(2,1)}), bf16[5,768,768]{2,1,0:T(8,128)(2,1)}) %all-gather.2.cloned.1.call-update) | async-done | bytes 5898256 | tf_op jit(solution)/shard_map/all_gather | solution.py:82
  258.8 0.0 copy-start.2
  258.8 1.9 fusion.2
  260.7 1.9 convolution_add_fusion.3
  262.6 0.0 copy-done.2
  262.6 0.5 convolution_add_fusion.2
  263.1 0.0 collective-permute-done.1
  263.1 0.5 convolution_add_fusion.1
  263.7 1.3 fusion.1
  (5 shorter events, 0.1 us)
Async XLA Ops:
  7.2 94.5 %copy-start = (bf16[768,768]{1,0:T(8,128)(2,1)S(1)}, bf16[768,768]{1,0:T(8,128)(2,1)}, u32[]{:S(2)}) copy-start(bf16[768,768]{1,0:T(8,128)(2,1)} %param.11) | copy-start | bytes 3538948
  8.5 7.0 %copy-start.4 = (s32[1,1,2,128]{3,2,1,0:T(2,128)S(1)}, s32[1,1,2,128]{3,2,1,0:T(2,128)}, u32[]{:S(2)}) copy-start(s32[1,1,2,128]{3,2,1,0:T(2,128)} %param.13) | copy-start | bytes 3076
  11.1 5.6 %copy-start.5 = (s32[1,2,2]{2,1,0:T(2,128)S(1)}, s32[1,2,2]{2,1,0:T(2,128)}, u32[]{:S(2)}) copy-start(s32[1,2,2]{2,1,0:T(2,128)} %param.15) | copy-start | bytes 52
  11.1 5.8 %copy-start.6 = (f32[1,1,2,128]{3,2,1,0:T(2,128)S(1)}, f32[1,1,2,128]{3,2,1,0:T(2,128)}, u32[]{:S(2)}) copy-start(f32[1,1,2,128]{3,2,1,0:T(2,128)} %param.14) | copy-start | bytes 3076
  11.1 11.6 %all-to-all-start.1 = ((bf16[2,128,768]{2,1,0:T(8,128)(2,1)}), bf16[2,128,768]{2,1,0:T(8,128)(2,1)S(1)}, u32[]{:S(2)}, u32[]{:S(2)}) async-start(bf16[2,128,768]{2,1,0:T(8,128)(2,1)} %bitcast.9), calls=%async_computation.1 | async-start | bytes 786432 | tf_op jit(solution)/shard_map/all_to_all | solution.py:50
  15.4 78.7 %all-reduce.3.cloned.1.call-start = ((), (), s32[]{:S(2)}) async-start(), calls=%async_computation.4 | async-start | bytes 4718592 | tf_op jit(solution)/shard_map/psum | solution.py:90
  24.7 70.2 %copy-start.3 = (bf16[1,256,384]{2,1,0:T(8,128)(2,1)S(1)}, bf16[1,256,384]{2,1,0:T(8,128)(2,1)}, u32[]{:S(2)}) copy-start(bf16[1,256,384]{2,1,0:T(8,128)(2,1)} %param.9) | copy-start | bytes 589828
  24.7 172.6 %all-reduce.5.cloned.1.call-start = ((), (), s32[]{:S(2)}) async-start(), calls=%async_computation.5 | async-start | bytes 4718592 | tf_op jit(solution)/shard_map/psum | solution.py:90
  94.1 164.6 %all-gather.2.cloned.1.call-start = ((), (), s32[]{:S(2)}) async-start(), calls=%async_computation.3 | async-start | bytes 6266880 | tf_op jit(solution)/shard_map/all_gather | solution.py:82
  98.2 8.2 %all-to-all-start = ((bf16[2,2,24576]{2,1,0:T(2,128)(2,1)}), bf16[2,2,24576]{2,1,0:T(2,128)(2,1)S(1)}, u32[]{:S(2)}, u32[]{:S(2)}) async-start(bf16[2,2,24576]{2,1,0:T(2,128)(2,1)} %reshape.152), calls=%async_computation | async-start | bytes 393216 | tf_op jit(solution)/shard_map/all_to_all | solution.py:46
  106.5 10.1 %all-to-all-start.2 = ((bf16[2,128,768]{2,1,0:T(8,128)(2,1)}), bf16[2,128,768]{2,1,0:T(8,128)(2,1)}, u32[]{:S(2)}, u32[]{:S(2)}) async-start(bf16[2,128,768]{2,1,0:T(8,128)(2,1)} %bitcast.13), calls=%async_computation.2 | async-start | bytes 786432 | tf_op jit(solution)/shard_map/all_to_all | solution.py:67
  112.6 7.1 %copy-start.1 = (bf16[1,256,768]{2,1,0:T(8,128)(2,1)S(1)}, bf16[1,256,768]{2,1,0:T(8,128)(2,1)}, u32[]{:S(2)}) copy-start(bf16[1,256,768]{2,1,0:T(8,128)(2,1)} %param.8) | copy-start | bytes 1179652
  120.1 80.6 %collective-permute-start = (bf16[1,2,768]{2,1,0:T(2,128)(2,1)S(1)}, bf16[1,2,768]{2,1,0:T(2,128)(2,1)S(1)}, u32[]{:S(2)}, u32[]{:S(2)}) collective-permute-start(bf16[1,2,768]{2,1,0:T(2,128)(2,1)S(1)} %get-tuple-element.3), channel_id=1, source_target_pairs={{1,0},{3,2},{5,4},{7,6},{9,8},{11,10},{13,12},{15,14},{17,16},{19,... | collective-permute-start | bytes 9224 | tf_op jit(solution)/shard_map/ppermute | solution.py:16
  121.4 141.8 %collective-permute-start.1 = (bf16[1,2,768]{2,1,0:T(2,128)(2,1)S(1)}, bf16[1,2,768]{2,1,0:T(2,128)(2,1)S(1)}, u32[]{:S(2)}, u32[]{:S(2)}) collective-permute-start(bf16[1,2,768]{2,1,0:T(2,128)(2,1)S(1)} %get-tuple-element.2), channel_id=1, source_target_pairs={{0,1},{2,3},{4,5},{6,7},{8,9},{10,11},{12,13},{14,15},{16,17},{18,... | collective-permute-start | bytes 9224 | tf_op jit(solution)/shard_map/ppermute | solution.py:15
  258.8 3.9 %copy-start.2 = (bf16[5,768,768]{2,1,0:T(8,128)(2,1)S(1)}, bf16[5,768,768]{2,1,0:T(8,128)(2,1)}, u32[]{:S(2)}) copy-start(bf16[5,768,768]{2,1,0:T(8,128)(2,1)} %all-gather.2.cloned.1.call-done) | copy-start | bytes 17694724
Sparse Core Ops, SparseCore 0:
  24.9 69.1 all-reduce.2
  98.1 99.2 all-reduce.4
  199.9 58.7 all-gather.1
